TPU v7x, 32 devices: a whole 2x2x4 slice. The times are simulated.
32 devices in a mesh: front: 4 (over y, core), row: 8 (over z, x).
Axes of the slice: x: 2, y: 2, z: 4, core: 2. Of those that a mesh axis runs over, the one named last changes fastest.
Arguments:
- rhs_diag: float32 [4, 32, 2048], P('front', None, 'row'), may hold values from -6 to 6
- rhs_off: float32 [4, 32, 12288], P('front', None, 'row'), may hold values from -6 to 6
- diag_factor: float32 [4, 2048, 2048], P('front', 'row'), may hold values from -0.125 to 0.125
- off_factor: float32 [4, 12288, 2048], P('front', 'row'), may hold values from -0.125 to 0.125
- diag_inverse: float32 [4, 4, 512, 512], P('front')
- pattern: int32 [4, 4, 96], P('front', None, 'row'), may hold values 0 or 1
- upd_vals: float32 [32, 4, 8, 4, 8, 128], P(None, 'front', 'row'), may hold values from -4 to 4
- upd_rows: int32 [4, 8, 4, 8, 128], P('front', 'row'), may hold values from 0 to 1791
Outputs:
- solved: float32 [4, 32, 2048], P('front', None, 'row')
- remainder: float32 [4, 32, 12288], P('front', None, 'row')
Inputs may be any that keep to these rules, and one draw needn't show every extreme that they name: `upd_rows`: relative rows of the receiving row block: below 256 a window row, else a row below the window; several entries may name one row.
All inputs are finite; a program needn't handle non-finite values. No bound on the sum of `pattern` on one device may be relied on, other than what follows from the above.
Results may differ from a plain program's by a relative error of at most 0.0001.
Values sent between devices are 32-bit elements; how exact they have to be, the bound alone decides.
A program may use at most 128 MiB of HBM per device.

v0:
```python
import jax
import jax.numpy as jnp
from jax import lax
from jax.sharding import PartitionSpec as P

W = 512
P_SIZE = 4
BR = 128


def local(rhs_diag, rhs_off, diag_factor, off_factor, diag_inverse, pattern, upd_vals, upd_rows):
    own_rows = diag_factor.shape[1]
    nrhs_count = upd_vals.shape[0]
    fronts_all = upd_vals.shape[3]
    groups_all = upd_vals.shape[4]
    slot_count = upd_vals.shape[5]
    flat_vals = upd_vals.reshape(nrhs_count, 1, fronts_all * groups_all, slot_count)
    arrived = lax.all_to_all(flat_vals, ("front", "row"), split_axis=2, concat_axis=1, tiled=True)
    received = arrived.reshape(nrhs_count, -1)
    targets = upd_rows.reshape(-1)
    combined = jnp.concatenate([rhs_diag[0], rhs_off[0]], axis=1)
    combined = combined.at[:, targets].add(received)
    upper = combined[:, :own_rows]
    lower = combined[:, own_rows:]
    diag_local = diag_factor[0]
    off_local = off_factor[0]
    inverse = diag_inverse[0]
    mask_rows = jnp.repeat(pattern[0].astype(jnp.float32), BR, axis=1)
    group = lax.axis_index("row")
    positions = group * own_rows + lax.iota(jnp.int32, own_rows)
    columns = lax.iota(jnp.int32, W)
    highest = lax.Precision.HIGHEST
    contract = (((1,), (1,)), ((), ()))
    pieces = []
    for panel in range(P_SIZE):
        picker = (
            (positions[:, None] // W == panel) & (positions[:, None] % W == columns[None, :])
        ).astype(jnp.float32)
        partial_rhs = jnp.dot(upper, picker, precision=highest, preferred_element_type=jnp.float32)
        panel_rhs = lax.psum(partial_rhs, "row")
        piece = lax.dot_general(
            panel_rhs,
            inverse[panel],
            contract,
            precision=highest,
            preferred_element_type=jnp.float32,
        )
        pieces.append(piece)
        upper = upper - lax.dot_general(
            piece,
            diag_local[:, panel * W : (panel + 1) * W],
            contract,
            precision=highest,
            preferred_element_type=jnp.float32,
        )
        term = lax.dot_general(
            piece,
            off_local[:, panel * W : (panel + 1) * W],
            contract,
            precision=highest,
            preferred_element_type=jnp.float32,
        )
        lower = lower - term * mask_rows[panel][None, :]
    solution = jnp.concatenate(pieces, axis=1)
    own_solution = lax.dynamic_slice_in_dim(solution, group * own_rows, own_rows, 1)
    return (own_solution[None], lower[None])


def solution(mesh):
    in_specs = (
        P("front", None, "row"),
        P("front", None, "row"),
        P("front", "row", None),
        P("front", "row", None),
        P("front", None, None, None),
        P("front", None, "row"),
        P(None, "front", "row", None, None, None),
        P("front", "row", None, None, None),
    )
    out_specs = (P("front", None, "row"), P("front", None, "row"))
    return jax.shard_map(local, mesh=mesh, in_specs=in_specs, out_specs=out_specs, check_vma=False)
```

profile of v0, /device:TPU:0, one launch (start us, length us, event | category | flops | bytes accessed | tf_op | source)
XLA Modules:
  0.0 367.9 jit_solution(12900171675111309321)
XLA Ops:
  7.2 2.1 copy.19
  9.3 7.3 %all-to-all-start = ((f32[32,1,32,128]{3,0,1,2:T(8,128)}), f32[32,1,32,128]{3,0,1,2:T(8,128)S(1)}, u32[]{:S(2)}, u32[]{:S(2)}) async-start(f32[32,1,32,128]{3,0,1,2:T(8,128)} %bitcast.4), calls=%async_computation | async-start | bytes 1048576 | tf_op jit(solution)/shard_map/all_to_all | solution.py:18
  16.6 0.0 all-reduce.5.cloned.1.call-start
  16.7 0.5 broadcast_compare_fusion.2
  17.2 0.7 convert_element_type.3
  17.9 0.9 pad_maximum_fusion
  18.9 0.7 broadcast_bitcast_fusion
  19.5 0.7 broadcast_bitcast_fusion.2
  20.2 0.5 broadcast_compare_fusion.4
  20.7 0.3 copy.21
  21.0 0.6 and_select_fusion
  21.6 0.7 compare_select_fusion
  22.3 10.5 %all-to-all-done = f32[32,1,32,128]{3,0,1,2:T(8,128)S(1)} async-done(((f32[32,1,32,128]{3,0,1,2:T(8,128)}), f32[32,1,32,128]{3,0,1,2:T(8,128)S(1)}, u32[]{:S(2)}, u32[]{:S(2)}) %all-to-all-start) | async-done | bytes 524320 | tf_op jit(solution)/shard_map/all_to_all | solution.py:18
  32.9 0.3 copy.20
  33.2 0.3 copy.29
  33.5 0.6 copy.22
  34.1 0.0 copy-start.7
  34.1 22.7 %scatter_fusion = f32[32,1792]{0,1:T(8,128)S(1)} fusion(f32[32,1792]{0,1:T(8,128)S(1)} %copy.21, s32[4096]{0:T(1024)S(1)} %bitcast.72, f32[4096,32]{1,0:T(8,128)S(1)} %copy.22), kind=kCustom, calls=%fused_computation | custom fusion | flops 131072 | bytes 1589248 | tf_op jit(solution)/shard_map/scatter-add | solution.py:22
  56.9 1.0 fusion.54
  57.9 0.0 all-reduce.5.cloned.1.call-update
  57.9 0.0 all-reduce.7.cloned.1.call-start
  58.0 0.1 copy.25
  58.1 67.0 %all-reduce.5.cloned.1.call-done = f32[32,512]{1,0:T(8,128)} async-done(((f32[32,512]{1,0:T(8,128)}), f32[32,512]{1,0:T(8,128)}) %all-reduce.5.cloned.1.call-update) | async-done | bytes 65552 | tf_op jit(solution)/shard_map/psum | solution.py:40
  125.1 2.3 fusion.41
  127.4 1.6 convolution_subtract_fusion.2
  129.0 1.0 fusion.56
  130.0 0.0 all-reduce.7.cloned.1.call-update
  130.1 0.0 all-reduce.9.cloned.1.call-start
  130.1 0.1 slice.100
  130.2 0.2 copy.26
  130.4 69.0 %all-reduce.7.cloned.1.call-done = f32[32,512]{1,0:T(8,128)} async-done(((f32[32,512]{1,0:T(8,128)}), f32[32,512]{1,0:T(8,128)}) %all-reduce.7.cloned.1.call-update) | async-done | bytes 65552 | tf_op jit(solution)/shard_map/psum | solution.py:40
  199.4 2.3 fusion.39
  201.7 1.6 convolution_subtract_fusion.1
  203.4 1.0 fusion.58
  204.4 0.0 all-reduce.9.cloned.1.call-update
  204.4 0.2 all-reduce.11.cloned.1.call-start
  204.6 4.8 %fusion.23 = f32[32,1536]{1,0:T(8,128)S(1)} fusion(f32[32,512]{1,0:T(8,128)S(1)} %fusion.39, f32[1536,2048]{1,0:T(8,128)} %bitcast.62, f32[1536]{0:T(1024)S(1)} %copy-done.3), kind=kOutput, calls=%fused_computation.14 | convolution fusion | flops 302039040 | bytes 3414016 | tf_op jit(solution)/shard_map/dot_general | solution.py:56
  209.4 64.3 %all-reduce.9.cloned.1.call-done = f32[32,512]{1,0:T(8,128)} async-done(((f32[32,512]{1,0:T(8,128)}), f32[32,512]{1,0:T(8,128)}) %all-reduce.9.cloned.1.call-update) | async-done | bytes 65552 | tf_op jit(solution)/shard_map/psum | solution.py:40
  273.7 2.3 fusion.37
  276.1 1.6 convolution_subtract_fusion
  277.7 1.0 fusion.60
  278.7 0.0 all-reduce.11.cloned.1.call-update
  278.7 4.8 %fusion.26 = f32[32,1536]{1,0:T(8,128)S(1)} fusion(f32[32,512]{1,0:T(8,128)S(1)} %fusion.37, f32[1536,2048]{1,0:T(8,128)} %bitcast.63, f32[1536]{0:T(1024)S(1)} %copy-done.2), kind=kOutput, calls=%fused_computation.15 | convolution fusion | flops 302039040 | bytes 3414016 | tf_op jit(solution)/shard_map/dot_general | solution.py:56
  283.5 64.5 %all-reduce.11.cloned.1.call-done = f32[32,512]{1,0:T(8,128)} async-done(((f32[32,512]{1,0:T(8,128)}), f32[32,512]{1,0:T(8,128)}) %all-reduce.11.cloned.1.call-update) | async-done | bytes 65552 | tf_op jit(solution)/shard_map/psum | solution.py:40
  348.1 2.3 fusion.35
  350.4 4.8 %fusion.29 = f32[32,1536]{1,0:T(8,128)S(1)} fusion(f32[32,512]{1,0:T(8,128)S(1)} %fusion.35, f32[1536,2048]{1,0:T(8,128)} %bitcast.64, f32[1536]{0:T(1024)S(1)} %copy-done.1), kind=kOutput, calls=%fused_computation.16 | convolution fusion | flops 302039040 | bytes 3414016 | tf_op jit(solution)/shard_map/dot_general | solution.py:56
  355.2 0.6 fusion.73
  355.8 5.5 %fusion.32 = f32[1,32,1536]{2,1,0:T(8,128)} fusion(f32[32,1536]{1,0:T(8,128)S(1)} %fusion.29, f32[32,1536]{1,0:T(8,128)S(1)} %fusion.26, f32[32,1536]{1,0:T(8,128)S(1)} %fusion.23, f32[32,1536]{1,0:T(8,128)S(1)} %copy.26, f32[32,512]{1,0:T(8,128)S(1)} %fusion.41, f32[1536,2048]{1,0:T(8,128)} %bitcast.65, f32[1536]{0:T(1024)S(1)} %copy-done), kind=kOutput, calls=%fused_computation.17 | convolution fusion | flops 302235648 | bytes 4200448 | tf_op jit(solution)/shard_map/dot_general | solution.py:56
  (19 shorter events, 0.1 us)
Async XLA Ops:
  9.3 23.6 %all-to-all-start = ((f32[32,1,32,128]{3,0,1,2:T(8,128)}), f32[32,1,32,128]{3,0,1,2:T(8,128)S(1)}, u32[]{:S(2)}, u32[]{:S(2)}) async-start(f32[32,1,32,128]{3,0,1,2:T(8,128)} %bitcast.4), calls=%async_computation | async-start | bytes 1048576 | tf_op jit(solution)/shard_map/all_to_all | solution.py:18
  16.6 108.5 %all-reduce.5.cloned.1.call-start = ((), (), s32[]{:S(2)}) async-start(), calls=%async_computation.1 | async-start | bytes 131072 | tf_op jit(solution)/shard_map/psum | solution.py:40
  34.1 22.8 %copy-start.4 = (s32[256]{0:T(256)S(1)}, s32[256]{0:T(256)}, u32[]{:S(2)}) copy-start(s32[256]{0:T(256)} %and_select_fusion) | copy-start | bytes 3076
  34.1 22.8 %copy-start.7 = (pred[256]{0:T(512)(128)(4,1)S(1)}, pred[256]{0:T(512)(128)(4,1)}, u32[]{:S(2)}) copy-start(pred[256]{0:T(512)(128)(4,1)} %broadcast_compare_fusion.2) | copy-start | bytes 772
  34.1 94.9 %copy-start.6 = (pred[256]{0:T(512)(128)(4,1)S(1)}, pred[256]{0:T(512)(128)(4,1)}, u32[]{:S(2)}) copy-start(pred[256]{0:T(512)(128)(4,1)} %broadcast_compare_fusion.4) | copy-start | bytes 772
  56.9 146.5 %copy-start.5 = (s32[256]{0:T(256)S(1)}, s32[256]{0:T(256)}, u32[]{:S(2)}) copy-start(s32[256]{0:T(256)} %and_select_fusion) | copy-start | bytes 3076
  56.9 147.7 %copy-start.3 = (f32[1536]{0:T(1024)S(1)}, f32[1536]{0:T(1024)}, u32[]{:S(2)}) copy-start(f32[1536]{0:T(1024)} %get-tuple-element.8) | copy-start | bytes 18436
  57.9 141.5 %all-reduce.7.cloned.1.call-start = ((), (), s32[]{:S(2)}) async-start(), calls=%async_computation.2 | async-start | bytes 131072 | tf_op jit(solution)/shard_map/psum | solution.py:40
  130.1 143.7 %all-reduce.9.cloned.1.call-start = ((), (), s32[]{:S(2)}) async-start(), calls=%async_computation.3 | async-start | bytes 131072 | tf_op jit(solution)/shard_map/psum | solution.py:40
  130.2 148.5 %copy-start.2 = (f32[1536]{0:T(1024)S(1)}, f32[1536]{0:T(1024)}, u32[]{:S(2)}) copy-start(f32[1536]{0:T(1024)} %get-tuple-element.7) | copy-start | bytes 18436
  204.4 143.7 %all-reduce.11.cloned.1.call-start = ((), (), s32[]{:S(2)}) async-start(), calls=%async_computation.4 | async-start | bytes 131072 | tf_op jit(solution)/shard_map/psum | solution.py:40
  209.4 140.9 %copy-start.1 = (f32[1536]{0:T(1024)S(1)}, f32[1536]{0:T(1024)}, u32[]{:S(2)}) copy-start(f32[1536]{0:T(1024)} %get-tuple-element.6) | copy-start | bytes 18436
  278.7 77.2 %copy-start = (f32[1536]{0:T(1024)S(1)}, f32[1536]{0:T(1024)}, u32[]{:S(2)}) copy-start(f32[1536]{0:T(1024)} %get-tuple-element.9) | copy-start | bytes 18436
Sparse Core Ops, SparseCore 0:
  58.0 66.9 all-reduce.4
  130.2 69.1 all-reduce.6
  204.5 69.1 all-reduce.8
  278.8 69.1 all-reduce.10
where the time goes:
time: 369 us; the launch traced here: 368 us
  waiting for transfers between devices  275 us (75%)
  matrix products  37.9 us (10%)
  other arithmetic  27.4 us (7%)
  between operations  14 us (4%)
  starting transfers between devices  7.67 us (2%)
  local copies, waits for them, and re-layouts  5.4 us (1%)
    psum x4, waiting for transfers between devices, local(): panel_rhs = lax.psum(partial_rhs, 'row')  265 us
    scatter-add x1, other arithmetic, local(): combined = combined.at[:, targets].add(received)  22.7 us
    dot_general x4, matrix products, local(): lax.dot_general(piece, off_local[:, panel * W:(panel + 1) * W], contract,...  19.9 us
    all_to_all x1, waiting for transfers between devices, local(): lax.all_to_all(flat_vals, ('front', 'row'), split_axis=2, concat_axis=1,...  10.5 us
    dot_general x4, matrix products, local(): lax.dot_general(panel_rhs, inverse[panel], contract, precision=highest, p...  9.18 us
  transfers between devices with their start and end apart: 5, of which 5 were waited for; matrix products, arithmetic and copies ran while one was open for 4% of the time, Pallas kernels for 0%

commit v1 on v0

--- a/solution.py
+++ b/solution.py
@@ -37,7 +37,11 @@
             (positions[:, None] // W == panel) & (positions[:, None] % W == columns[None, :])
         ).astype(jnp.float32)
         partial_rhs = jnp.dot(upper, picker, precision=highest, preferred_element_type=jnp.float32)
-        panel_rhs = lax.psum(partial_rhs, "row")
+        panel_rhs = partial_rhs
+        for hop in (1, 2, 4):
+            panel_rhs = panel_rhs + lax.ppermute(
+                panel_rhs, "row", [(dev, dev ^ hop) for dev in range(8)]
+            )
         piece = lax.dot_general(
             panel_rhs,
             inverse[panel],

time: 369 us -> 137 us (0.37)
  waiting for transfers between devices: 275 us -> 56.1 us
  between operations: 14 us -> 0.94 us
  starting transfers between devices: 7.67 us -> 12.8 us
    psum x4 -> x0, waiting for transfers between devices: 265 us -> none  [local(): panel_rhs = lax.psum(partial_rhs, 'row')]
    ppermute x0 -> x12, waiting for transfers between devices: none -> 43 us  [local(): lax.ppermute(panel_rhs, 'row', [(dev, dev ^ hop) for dev in range(8)])]
    ppermute x0 -> x12, starting transfers between devices: none -> 5.45 us  [local(): lax.ppermute(panel_rhs, 'row', [(dev, dev ^ hop) for dev in range(8)])]
  transfers between devices with their start and end apart: 5 -> 13, of which waited for: 5 -> 11; matrix products, arithmetic and copies ran while one was open for 4% -> 10% of each run, Pallas kernels for 0% -> 0%
where the time goes in v1:
time: 137 us; the launch traced here: 136 us
  waiting for transfers between devices  56.1 us (41%)
  matrix products  34.8 us (25%)
  other arithmetic  27.1 us (20%)
  starting transfers between devices  12.8 us (9%)
  local copies, waits for them, and re-layouts  4.24 us (3%)
    ppermute x12, waiting for transfers between devices, local(): lax.ppermute(panel_rhs, 'row', [(dev, dev ^ hop) for dev in range(8)])  43 us
    scatter-add x1, other arithmetic, local(): combined = combined.at[:, targets].add(received)  22.9 us
    dot_general x4, matrix products, local(): lax.dot_general(piece, off_local[:, panel * W:(panel + 1) * W], contract,...  20.1 us
    all_to_all x1, waiting for transfers between devices, local(): lax.all_to_all(flat_vals, ('front', 'row'), split_axis=2, concat_axis=1,...  13.1 us
    dot_general x4, matrix products, local(): lax.dot_general(panel_rhs, inverse[panel], contract, precision=highest, p...  9.03 us
    all_to_all x1, starting transfers between devices, local(): lax.all_to_all(flat_vals, ('front', 'row'), split_axis=2, concat_axis=1,...  7.33 us
    ppermute x12, starting transfers between devices, local(): lax.ppermute(panel_rhs, 'row', [(dev, dev ^ hop) for dev in range(8)])  5.45 us
    dot_general x4, matrix products, local(): jnp.dot(upper, picker, precision=highest, preferred_element_type=jnp.floa...  2.97 us
  transfers between devices with their start and end apart: 13, of which 11 were waited for; matrix products, arithmetic and copies ran while one was open for 10% of the time, Pallas kernels for 0%

profile of v1, /device:TPU:0, one launch (start us, length us, event | category | flops | bytes accessed | tf_op | source)
XLA Modules:
  0.0 136.1 jit_solution(16465550207153580345)
XLA Ops:
  0.6 2.1 %copy.19 = f32[32,1,1,4,8,128]{5,0,4,3,2,1:T(8,128)} copy(f32[32,1,1,4,8,128]{5,4,3,2,1,0:T(8,128)} %param.14) | data formatting | bytes 1048576 | tf_op args[6]
  2.8 7.3 %all-to-all-start = ((f32[32,1,32,128]{3,0,1,2:T(8,128)}), f32[32,1,32,128]{3,0,1,2:T(8,128)S(1)}, u32[]{:S(2)}, u32[]{:S(2)}) async-start(f32[32,1,32,128]{3,0,1,2:T(8,128)} %bitcast.4), calls=%async_computation | async-start | bytes 1048576 | tf_op jit(solution)/shard_map/all_to_all | solution.py:18
  10.1 0.9 pad_maximum_fusion
  11.1 0.5 broadcast_compare_fusion.2
  11.6 0.3 copy.21
  11.9 0.6 and_select_fusion
  12.5 0.7 compare_select_fusion
  13.2 13.1 %all-to-all-done = f32[32,1,32,128]{3,0,1,2:T(8,128)S(1)} async-done(((f32[32,1,32,128]{3,0,1,2:T(8,128)}), f32[32,1,32,128]{3,0,1,2:T(8,128)S(1)}, u32[]{:S(2)}, u32[]{:S(2)}) %all-to-all-start) | async-done | bytes 524320 | tf_op jit(solution)/shard_map/all_to_all | solution.py:18
  26.3 0.3 copy.20
  26.6 0.3 copy.29
  27.0 0.6 copy.22
  27.6 22.9 %scatter_fusion = f32[32,1792]{0,1:T(8,128)S(1)} fusion(f32[32,1792]{0,1:T(8,128)S(1)} %copy.21, s32[4096]{0:T(1024)S(1)} %bitcast.68, f32[4096,32]{1,0:T(8,128)S(1)} %copy.22), kind=kCustom, calls=%fused_computation | custom fusion | flops 131072 | bytes 1589248 | tf_op jit(solution)/shard_map/scatter-add | solution.py:22
  50.5 1.2 fusion.54
  51.7 1.0 collective-permute-start
  52.7 3.3 %collective-permute-done = f32[32,512]{1,0:T(8,128)S(1)} collective-permute-done((f32[32,512]{1,0:T(8,128)S(1)}, f32[32,512]{1,0:T(8,128)S(1)}, u32[]{:S(2)}, u32[]{:S(2)}) %collective-permute-start) | collective-permute-done | bytes 65568 | tf_op jit(solution)/shard_map/ppermute | solution.py:42
  56.0 0.8 collective-permute-start.1
  56.9 3.5 %collective-permute-done.1 = f32[32,512]{1,0:T(8,128)S(1)} collective-permute-done((f32[32,512]{1,0:T(8,128)S(1)}, f32[32,512]{1,0:T(8,128)S(1)}, u32[]{:S(2)}, u32[]{:S(2)}) %collective-permute-start.1) | collective-permute-done | bytes 65568 | tf_op jit(solution)/shard_map/ppermute | solution.py:42
  60.6 5.8 %collective-permute-done.2 = f32[32,512]{1,0:T(8,128)S(1)} collective-permute-done((f32[32,512]{1,0:T(8,128)S(1)}, f32[32,512]{1,0:T(8,128)S(1)}, u32[]{:S(2)}, u32[]{:S(2)}) %collective-permute-start.2) | collective-permute-done | bytes 65568 | tf_op jit(solution)/shard_map/ppermute | solution.py:42
  66.3 2.3 %fusion.41 = f32[32,512]{1,0:T(8,128)S(1)} fusion(f32[1,4,512,512]{3,2,1,0:T(8,128)} %param.12, f32[32,512]{1,0:T(8,128)S(1)} %add.114, f32[32,512]{1,0:T(8,128)S(1)} %collective-permute-done.2), kind=kOutput, calls=%fused_computation.27 | convolution fusion | flops 100679680 | bytes 1245184 | tf_op jit(solution)/shard_map/dot_general | solution.py:45
  68.6 1.6 %convolution_subtract_fusion.2 = f32[32,256]{1,0:T(8,128)S(1)} fusion(f32[32,256]{1,0:T(8,128)S(1)} %copy.25, f32[32,512]{1,0:T(8,128)S(1)} %fusion.41, f32[256,2048]{1,0:T(8,128)} %bitcast.64), kind=kOutput, calls=%fused_computation.20 | convolution fusion | flops 50339840 | bytes 655360 | tf_op jit(solution)/shard_map/dot_general | solution.py:53
  70.2 1.0 fusion.56
  71.3 0.4 collective-permute-start.3
  71.7 0.7 convert_element_type.3
  72.4 3.2 %collective-permute-done.3 = f32[32,512]{1,0:T(8,128)S(1)} collective-permute-done((f32[32,512]{1,0:T(8,128)S(1)}, f32[32,512]{1,0:T(8,128)S(1)}, u32[]{:S(2)}, u32[]{:S(2)}) %collective-permute-start.3) | collective-permute-done | bytes 65568 | tf_op jit(solution)/shard_map/ppermute | solution.py:42
  75.6 0.6 collective-permute-start.4
  76.2 3.7 %collective-permute-done.4 = f32[32,512]{1,0:T(8,128)S(1)} collective-permute-done((f32[32,512]{1,0:T(8,128)S(1)}, f32[32,512]{1,0:T(8,128)S(1)}, u32[]{:S(2)}, u32[]{:S(2)}) %collective-permute-start.4) | collective-permute-done | bytes 65568 | tf_op jit(solution)/shard_map/ppermute | solution.py:42
  80.0 5.8 %collective-permute-done.5 = f32[32,512]{1,0:T(8,128)S(1)} collective-permute-done((f32[32,512]{1,0:T(8,128)S(1)}, f32[32,512]{1,0:T(8,128)S(1)}, u32[]{:S(2)}, u32[]{:S(2)}) %collective-permute-start.5) | collective-permute-done | bytes 65568 | tf_op jit(solution)/shard_map/ppermute | solution.py:42
  85.9 2.3 %fusion.39 = f32[32,512]{1,0:T(8,128)S(1)} fusion(f32[1,4,512,512]{3,2,1,0:T(8,128)} %param.12, f32[32,512]{1,0:T(8,128)S(1)} %add.117, f32[32,512]{1,0:T(8,128)S(1)} %collective-permute-done.5), kind=kOutput, calls=%fused_computation.25 | convolution fusion | flops 100679680 | bytes 1245184 | tf_op jit(solution)/shard_map/dot_general | solution.py:45
  88.1 0.6 convolution_subtract_fusion.1
  88.7 0.4 fusion.58
  89.1 0.2 collective-permute-start.6
  89.4 4.1 %collective-permute-done.6 = f32[32,512]{1,0:T(8,128)S(1)} collective-permute-done((f32[32,512]{1,0:T(8,128)S(1)}, f32[32,512]{1,0:T(8,128)S(1)}, u32[]{:S(2)}, u32[]{:S(2)}) %collective-permute-start.6) | collective-permute-done | bytes 65568 | tf_op jit(solution)/shard_map/ppermute | solution.py:42
  93.6 4.2 %collective-permute-done.7 = f32[32,512]{1,0:T(8,128)S(1)} collective-permute-done((f32[32,512]{1,0:T(8,128)S(1)}, f32[32,512]{1,0:T(8,128)S(1)}, u32[]{:S(2)}, u32[]{:S(2)}) %collective-permute-start.7) | collective-permute-done | bytes 65568 | tf_op jit(solution)/shard_map/ppermute | solution.py:42
  97.9 5.6 %collective-permute-done.8 = f32[32,512]{1,0:T(8,128)S(1)} collective-permute-done((f32[32,512]{1,0:T(8,128)S(1)}, f32[32,512]{1,0:T(8,128)S(1)}, u32[]{:S(2)}, u32[]{:S(2)}) %collective-permute-start.8) | collective-permute-done | bytes 65568 | tf_op jit(solution)/shard_map/ppermute | solution.py:42
  103.5 2.3 %fusion.37 = f32[32,512]{1,0:T(8,128)S(1)} fusion(f32[1,4,512,512]{3,2,1,0:T(8,128)} %param.12, f32[32,512]{1,0:T(8,128)S(1)} %add.120, f32[32,512]{1,0:T(8,128)S(1)} %collective-permute-done.8), kind=kOutput, calls=%fused_computation.23 | convolution fusion | flops 100679680 | bytes 1245184 | tf_op jit(solution)/shard_map/dot_general | solution.py:45
  105.7 0.6 convolution_subtract_fusion
  106.3 0.4 fusion.60
  106.7 0.1 collective-permute-start.9
  106.9 0.2 copy.26
  107.1 3.9 %collective-permute-done.9 = f32[32,512]{1,0:T(8,128)S(1)} collective-permute-done((f32[32,512]{1,0:T(8,128)S(1)}, f32[32,512]{1,0:T(8,128)S(1)}, u32[]{:S(2)}, u32[]{:S(2)}) %collective-permute-start.9) | collective-permute-done | bytes 65568 | tf_op jit(solution)/shard_map/ppermute | solution.py:42
  111.0 0.2 collective-permute-start.10
  111.2 4.8 %fusion.23 = f32[32,1536]{1,0:T(8,128)S(1)} fusion(f32[32,512]{1,0:T(8,128)S(1)} %fusion.39, f32[1536,2048]{1,0:T(8,128)} %bitcast.58, f32[1536]{0:T(1024)S(1)} %broadcast_bitcast_fusion.2), kind=kOutput, calls=%fused_computation.14 | convolution fusion | flops 302039040 | bytes 3414016 | tf_op jit(solution)/shard_map/dot_general | solution.py:60
  116.0 1.8 %collective-permute-start.11 = (f32[32,512]{1,0:T(8,128)S(1)}, f32[32,512]{1,0:T(8,128)S(1)}, u32[]{:S(2)}, u32[]{:S(2)}) collective-permute-start(f32[32,512]{1,0:T(8,128)S(1)} %add.123), channel_id=1, source_target_pairs={{0,4},{1,5},{2,6},{3,7},{4,0},{5,1},{6,2},{7,3},{8,12},{9,13},{10,... | collective-permute-start | bytes 196616 | tf_op jit(solution)/shard_map/ppermute | solution.py:42
  117.8 4.8 %fusion.26 = f32[32,1536]{1,0:T(8,128)S(1)} fusion(f32[32,512]{1,0:T(8,128)S(1)} %fusion.37, f32[1536,2048]{1,0:T(8,128)} %bitcast.59, f32[1536]{0:T(1024)S(1)} %get-tuple-element.7), kind=kOutput, calls=%fused_computation.15 | convolution fusion | flops 302039040 | bytes 3414016 | tf_op jit(solution)/shard_map/dot_general | solution.py:60
  122.6 2.3 %fusion.35 = f32[32,512]{1,0:T(8,128)S(1)} fusion(f32[1,4,512,512]{3,2,1,0:T(8,128)} %param.12, f32[32,512]{1,0:T(8,128)S(1)} %add.123, f32[32,512]{1,0:T(8,128)S(1)} %collective-permute-done.11), kind=kOutput, calls=%fused_computation.21 | convolution fusion | flops 100679680 | bytes 1245184 | tf_op jit(solution)/shard_map/dot_general | solution.py:45
  124.9 5.0 %fusion.29 = f32[32,1536]{1,0:T(8,128)S(1)} fusion(f32[32,512]{1,0:T(8,128)S(1)} %fusion.35, f32[1536,2048]{1,0:T(8,128)} %bitcast.60, f32[1536]{0:T(1024)S(1)} %get-tuple-element.6), kind=kOutput, calls=%fused_computation.16 | convolution fusion | flops 302039040 | bytes 3414016 | tf_op jit(solution)/shard_map/dot_general | solution.py:60
  129.9 0.6 fusion.77
  130.6 5.5 %fusion.32 = f32[1,32,1536]{2,1,0:T(8,128)} fusion(f32[32,1536]{1,0:T(8,128)S(1)} %fusion.29, f32[32,1536]{1,0:T(8,128)S(1)} %fusion.26, f32[32,1536]{1,0:T(8,128)S(1)} %fusion.23, f32[32,1536]{1,0:T(8,128)S(1)} %copy.26, f32[32,512]{1,0:T(8,128)S(1)} %fusion.41, f32[1536,2048]{1,0:T(8,128)} %bitcast.61, f32[1536]{0:T(1024)S(1)} %broadcast_bitcast_fusion.3), kind=kOutput, calls=%fused_computation.17 | convolution fusion | flops 302235648 | bytes 4200448 | tf_op jit(solution)/shard_map/dot_general | solution.py:60
  (28 shorter events, 0.8 us)
Async XLA Ops:
  2.8 23.6 %all-to-all-start = ((f32[32,1,32,128]{3,0,1,2:T(8,128)}), f32[32,1,32,128]{3,0,1,2:T(8,128)S(1)}, u32[]{:S(2)}, u32[]{:S(2)}) async-start(f32[32,1,32,128]{3,0,1,2:T(8,128)} %bitcast.4), calls=%async_computation | async-start | bytes 1048576 | tf_op jit(solution)/shard_map/all_to_all | solution.py:18
  50.5 37.7 %copy-start = (f32[1,256,2048]{2,1,0:T(8,128)S(1)}, f32[1,256,2048]{2,1,0:T(8,128)}, u32[]{:S(2)}) copy-start(f32[1,256,2048]{2,1,0:T(8,128)} %param.10) | copy-start | bytes 6291460
  50.5 38.2 %copy-start.1 = (s32[256]{0:T(256)S(1)}, s32[256]{0:T(256)}, u32[]{:S(2)}) copy-start(s32[256]{0:T(256)} %and_select_fusion) | copy-start | bytes 3076
  51.7 4.3 %collective-permute-start = (f32[32,512]{1,0:T(8,128)S(1)}, f32[32,512]{1,0:T(8,128)S(1)}, u32[]{:S(2)}, u32[]{:S(2)}) collective-permute-start(f32[32,512]{1,0:T(8,128)S(1)} %fusion.54), channel_id=1, source_target_pairs={{0,1},{1,0},{2,3},{3,2},{4,5},{5,4},{6,7},{7,6},{8,9},{9,8},{10,11... | collective-permute-start | bytes 196616 | tf_op jit(solution)/shard_map/ppermute | solution.py:42
  56.0 4.3 %collective-permute-start.1 = (f32[32,512]{1,0:T(8,128)S(1)}, f32[32,512]{1,0:T(8,128)S(1)}, u32[]{:S(2)}, u32[]{:S(2)}) collective-permute-start(f32[32,512]{1,0:T(8,128)S(1)} %add.113), channel_id=1, source_target_pairs={{0,2},{1,3},{2,0},{3,1},{4,6},{5,7},{6,4},{7,5},{8,10},{9,11},{10,... | collective-permute-start | bytes 196616 | tf_op jit(solution)/shard_map/ppermute | solution.py:42
  60.4 5.9 %collective-permute-start.2 = (f32[32,512]{1,0:T(8,128)S(1)}, f32[32,512]{1,0:T(8,128)S(1)}, u32[]{:S(2)}, u32[]{:S(2)}) collective-permute-start(f32[32,512]{1,0:T(8,128)S(1)} %add.114), channel_id=1, source_target_pairs={{0,4},{1,5},{2,6},{3,7},{4,0},{5,1},{6,2},{7,3},{8,12},{9,13},{10,... | collective-permute-start | bytes 196616 | tf_op jit(solution)/shard_map/ppermute | solution.py:42
  71.3 4.3 %collective-permute-start.3 = (f32[32,512]{1,0:T(8,128)S(1)}, f32[32,512]{1,0:T(8,128)S(1)}, u32[]{:S(2)}, u32[]{:S(2)}) collective-permute-start(f32[32,512]{1,0:T(8,128)S(1)} %fusion.56), channel_id=1, source_target_pairs={{0,1},{1,0},{2,3},{3,2},{4,5},{5,4},{6,7},{7,6},{8,9},{9,8},{10,11... | collective-permute-start | bytes 196616 | tf_op jit(solution)/shard_map/ppermute | solution.py:42
  75.6 4.3 %collective-permute-start.4 = (f32[32,512]{1,0:T(8,128)S(1)}, f32[32,512]{1,0:T(8,128)S(1)}, u32[]{:S(2)}, u32[]{:S(2)}) collective-permute-start(f32[32,512]{1,0:T(8,128)S(1)} %add.116), channel_id=1, source_target_pairs={{0,2},{1,3},{2,0},{3,1},{4,6},{5,7},{6,4},{7,5},{8,10},{9,11},{10,... | collective-permute-start | bytes 196616 | tf_op jit(solution)/shard_map/ppermute | solution.py:42
  80.0 5.9 %collective-permute-start.5 = (f32[32,512]{1,0:T(8,128)S(1)}, f32[32,512]{1,0:T(8,128)S(1)}, u32[]{:S(2)}, u32[]{:S(2)}) collective-permute-start(f32[32,512]{1,0:T(8,128)S(1)} %add.117), channel_id=1, source_target_pairs={{0,4},{1,5},{2,6},{3,7},{4,0},{5,1},{6,2},{7,3},{8,12},{9,13},{10,... | collective-permute-start | bytes 196616 | tf_op jit(solution)/shard_map/ppermute | solution.py:42
  89.1 4.3 %collective-permute-start.6 = (f32[32,512]{1,0:T(8,128)S(1)}, f32[32,512]{1,0:T(8,128)S(1)}, u32[]{:S(2)}, u32[]{:S(2)}) collective-permute-start(f32[32,512]{1,0:T(8,128)S(1)} %fusion.58), channel_id=1, source_target_pairs={{0,1},{1,0},{2,3},{3,2},{4,5},{5,4},{6,7},{7,6},{8,9},{9,8},{10,11... | collective-permute-start | bytes 196616 | tf_op jit(solution)/shard_map/ppermute | solution.py:42
  93.5 4.3 %collective-permute-start.7 = (f32[32,512]{1,0:T(8,128)S(1)}, f32[32,512]{1,0:T(8,128)S(1)}, u32[]{:S(2)}, u32[]{:S(2)}) collective-permute-start(f32[32,512]{1,0:T(8,128)S(1)} %add.119), channel_id=1, source_target_pairs={{0,2},{1,3},{2,0},{3,1},{4,6},{5,7},{6,4},{7,5},{8,10},{9,11},{10,... | collective-permute-start | bytes 196616 | tf_op jit(solution)/shard_map/ppermute | solution.py:42
  97.8 5.7 %collective-permute-start.8 = (f32[32,512]{1,0:T(8,128)S(1)}, f32[32,512]{1,0:T(8,128)S(1)}, u32[]{:S(2)}, u32[]{:S(2)}) collective-permute-start(f32[32,512]{1,0:T(8,128)S(1)} %add.120), channel_id=1, source_target_pairs={{0,4},{1,5},{2,6},{3,7},{4,0},{5,1},{6,2},{7,3},{8,12},{9,13},{10,... | collective-permute-start | bytes 196616 | tf_op jit(solution)/shard_map/ppermute | solution.py:42
  106.7 4.3 %collective-permute-start.9 = (f32[32,512]{1,0:T(8,128)S(1)}, f32[32,512]{1,0:T(8,128)S(1)}, u32[]{:S(2)}, u32[]{:S(2)}) collective-permute-start(f32[32,512]{1,0:T(8,128)S(1)} %fusion.60), channel_id=1, source_target_pairs={{0,1},{1,0},{2,3},{3,2},{4,5},{5,4},{6,7},{7,6},{8,9},{9,8},{10,11... | collective-permute-start | bytes 196616 | tf_op jit(solution)/shard_map/ppermute | solution.py:42
  111.0 5.0 %collective-permute-start.10 = (f32[32,512]{1,0:T(8,128)S(1)}, f32[32,512]{1,0:T(8,128)S(1)}, u32[]{:S(2)}, u32[]{:S(2)}) collective-permute-start(f32[32,512]{1,0:T(8,128)S(1)} %add.122), channel_id=1, source_target_pairs={{0,2},{1,3},{2,0},{3,1},{4,6},{5,7},{6,4},{7,5},{8,10},{9,11},{10,... | collective-permute-start | bytes 196616 | tf_op jit(solution)/shard_map/ppermute | solution.py:42
  116.0 6.6 %collective-permute-start.11 = (f32[32,512]{1,0:T(8,128)S(1)}, f32[32,512]{1,0:T(8,128)S(1)}, u32[]{:S(2)}, u32[]{:S(2)}) collective-permute-start(f32[32,512]{1,0:T(8,128)S(1)} %add.123), channel_id=1, source_target_pairs={{0,4},{1,5},{2,6},{3,7},{4,0},{5,1},{6,2},{7,3},{8,12},{9,13},{10,... | collective-permute-start | bytes 196616 | tf_op jit(solution)/shard_map/ppermute | solution.py:42
